TPU v7x, 32 devices: a whole 2x2x4 slice. The times are simulated.
32 devices in a mesh: trainer: 16 (over z, x, core), store: 2 (over y).
Axes of the slice: x: 2, y: 2, z: 4, core: 2. Of those that a mesh axis runs over, the one named last changes fastest.
Arguments:
- memory: float32 [256, 512], P('store'), may hold values from -240 to 240
- event_feats: bfloat16 [25600, 128], P('store'), may hold values from -6 to 6
- batch_rows: int32 [16, 64], P('trainer', 'store'), may hold values from 0 to 127, as said below
- target_time: int32 [16, 64], P('trainer', 'store'), may hold values from 1024 to 2047
- neighbor_owner: int32 [16, 64, 100, 1], P('trainer', 'store'), may hold values from 0 to 1; in each aligned block of 3200 rows (0 to 3199, 3200 to 6399, ..., all dimensions but the last counted through in order) at most 3200 rows name the same one
- neighbor_event: int32 [16, 64, 100], P('trainer', 'store'), may hold values from 0 to 12799
- neighbor_time: int32 [16, 64, 100], P('trainer', 'store'), may hold values from 0 to 1023, as said below
- time_freq: float32 [128], replicated, may hold values from 0.001 to 1
- time_phase: float32 [128], replicated, may hold values from -3.140625 to 3.140625
- w_query: bfloat16 [512, 512], replicated, may hold values from -0.25 to 0.25
- w_key: bfloat16 [256, 512], replicated, may hold values from -0.375 to 0.375
- w_value: bfloat16 [256, 512], replicated, may hold values from -0.375 to 0.375
- ln_gain: float32 [512], replicated, may hold values from 0.5 to 1.5
- gru_input: bfloat16 [256, 1536], replicated, may hold values from -0.375 to 0.375
- gru_hidden: bfloat16 [512, 1536], replicated, may hold values from -0.25 to 0.25
- emb_cotangent: bfloat16 [16, 64, 512], P('trainer', 'store'), may hold values from -6 to 6
Outputs:
- embedding: bfloat16 [16, 64, 512], P('trainer', 'store')
- memory_next: float32 [16, 256, 512], P('trainer', 'store')
- key_value_grad: float32 [262144], P(('trainer', 'store'))
Inputs may be any that keep to these rules, and one draw needn't show every extreme that they name: `batch_rows`: the 32 entries that one device holds are distinct. `neighbor_owner`: among the 3200 neighbor rows of one device, no owner is named by more than 3200 rows. `neighbor_time`: along the 100 neighbors of a target, times never rise.
All inputs are finite; a program needn't handle non-finite values.
Results may differ from a plain program's by a relative error of at most 0.003.
The roundings to bfloat16 on the way count: a program that leaves them out, or rounds other values in their place, can miss the bound.
Values may be sent and summed in bfloat16 or wider, within the bound.
No kernel may reach another device: no remote copies, remote signals or barrier semaphores. Data moves between devices by JAX's collectives and lax.ppermute only.
A program may use at most 64 MiB of HBM per device.

v0:
```python
import math
import jax
import jax.numpy as jnp
from jax import lax
from jax.sharding import PartitionSpec as P

HEADS = 2
highest = lax.Precision.HIGHEST


def passed_along(value, axis, steps):
    count = lax.axis_size(axis)
    pairs = [(source, (source + steps) % count) for source in range(count)]
    return lax.ppermute(value, axis, pairs)


def key_inputs_of(feature_rows, target_times, neighbor_times, time_freq, time_phase):
    elapsed = (target_times[:, None] - neighbor_times).astype(jnp.float32)
    encoded = jnp.cos(elapsed[:, :, None] * time_freq + time_phase)
    return jnp.concatenate([feature_rows, encoded.astype(jnp.bfloat16)], axis=-1)


def memory_step(mem_rows, mem_low, latest_inputs, gru_input, gru_hidden):
    mem_width = mem_rows.shape[1]
    from_input = jnp.dot(latest_inputs, gru_input, preferred_element_type=jnp.float32)
    from_state = jnp.dot(mem_low, gru_hidden, preferred_element_type=jnp.float32)
    update_gate = jax.nn.sigmoid(from_input[:, :mem_width] + from_state[:, :mem_width])
    reset_gate = jax.nn.sigmoid(
        from_input[:, mem_width : 2 * mem_width] + from_state[:, mem_width : 2 * mem_width]
    )
    candidate = jnp.tanh(
        from_input[:, 2 * mem_width :] + reset_gate * from_state[:, 2 * mem_width :]
    )
    return (1.0 - update_gate) * candidate + update_gate * mem_rows


def attend_block(mem_rows, query, key_inputs, cotangent, w_key, w_value, ln_gain):
    block_size, neighbors, in_width = key_inputs.shape
    mem_width = w_key.shape[1]
    head_dim = mem_width // HEADS
    flat_inputs = key_inputs.reshape(block_size * neighbors, in_width)
    key_rows = jnp.dot(flat_inputs, w_key, preferred_element_type=jnp.float32).reshape(
        block_size, neighbors, HEADS, head_dim
    )
    value_rows = jnp.dot(flat_inputs, w_value, preferred_element_type=jnp.float32).reshape(
        block_size, neighbors, HEADS, head_dim
    )
    query_heads = query.reshape(block_size, HEADS, head_dim)
    score_scale = 1.0 / math.sqrt(head_dim)
    scores = jnp.einsum("bhd,bkhd->bhk", query_heads, key_rows, precision=highest) * score_scale
    row_max = jnp.max(scores, axis=-1, keepdims=True)
    exponent = jnp.exp(scores - row_max)
    attention = exponent / jnp.sum(exponent, axis=-1, keepdims=True)
    aggregate = jnp.einsum("bhk,bkhd->bhd", attention, value_rows, precision=highest).reshape(
        block_size, mem_width
    )
    summed = aggregate + mem_rows
    centered = summed - jnp.mean(summed, axis=-1, keepdims=True)
    inv_std = lax.rsqrt(jnp.mean(centered * centered, axis=-1, keepdims=True) + 1e-05)
    normed = centered * inv_std
    embedded = normed * ln_gain
    grad_normed = cotangent * ln_gain
    grad_summed = (
        grad_normed
        - jnp.mean(grad_normed, axis=-1, keepdims=True)
        - normed * jnp.mean(grad_normed * normed, axis=-1, keepdims=True)
    ) * inv_std
    grad_heads = grad_summed.reshape(block_size, HEADS, head_dim)
    grad_values = jnp.einsum("bhk,bhd->bkhd", attention, grad_heads, precision=highest)
    grad_attention = jnp.einsum("bhd,bkhd->bhk", grad_heads, value_rows, precision=highest)
    grad_scores = attention * (
        grad_attention - jnp.sum(attention * grad_attention, axis=-1, keepdims=True)
    )
    grad_keys = (
        jnp.einsum("bhk,bhd->bkhd", grad_scores, query_heads, precision=highest) * score_scale
    )
    contract = (((0,), (0,)), ((), ()))
    grad_key = lax.dot_general(
        flat_inputs,
        grad_keys.reshape(block_size * neighbors, mem_width).astype(jnp.bfloat16),
        contract,
        preferred_element_type=jnp.float32,
    )
    grad_value = lax.dot_general(
        flat_inputs,
        grad_values.reshape(block_size * neighbors, mem_width).astype(jnp.bfloat16),
        contract,
        preferred_element_type=jnp.float32,
    )
    return (embedded, jnp.stack([grad_key, grad_value]))


def on_device(
    memory,
    event_feats,
    batch_rows,
    target_time,
    neighbor_owner,
    neighbor_event,
    neighbor_time,
    time_freq,
    time_phase,
    w_query,
    w_key,
    w_value,
    ln_gain,
    gru_input,
    gru_hidden,
    emb_cotangent,
):
    targets = batch_rows.shape[1]
    neighbors = neighbor_event.shape[2]
    mem_width = memory.shape[1]
    held_rows = event_feats.shape[0]
    feat_width = event_feats.shape[1]
    total_rows = targets * neighbors
    owners = neighbor_owner.reshape(total_rows)
    local_ids = neighbor_event.reshape(total_rows)
    wanted = owners * held_rows + local_ids
    blank_rows = jnp.zeros((total_rows, feat_width), jnp.bfloat16)
    shard_rows = lax.all_gather(event_feats, "store", axis=0, tiled=True)
    offset = jnp.int32(0)
    shard_len = shard_rows.shape[0]
    inside = (wanted >= offset) & (wanted < offset + shard_len)
    position = jnp.clip(wanted, 0, shard_len - 1)
    feature_rows = jnp.where(inside[:, None], jnp.take(shard_rows, position, axis=0), blank_rows)
    target_rows = batch_rows[0]
    mem_rows = memory[target_rows]
    mem_low = mem_rows.astype(jnp.bfloat16)
    key_inputs = key_inputs_of(
        feature_rows.reshape(targets, neighbors, feat_width),
        target_time[0],
        neighbor_time[0],
        time_freq,
        time_phase,
    )
    new_rows = memory_step(mem_rows, mem_low, key_inputs[:, 0, :], gru_input, gru_hidden)
    memory_next = passed_along(memory.at[target_rows].set(new_rows), "trainer", 1)
    query = jnp.dot(mem_low, w_query, preferred_element_type=jnp.float32)
    replicas = lax.axis_size("trainer") * lax.axis_size("store")
    cotangent = emb_cotangent[0].astype(jnp.float32) * (1.0 / math.sqrt(replicas))
    block_size = math.gcd(targets, 8)
    blocks = targets // block_size

    def one_block(carried, inputs):
        rows_here, query_here, inputs_here, cot_here = inputs
        embedded, grads = attend_block(
            rows_here, query_here, inputs_here, cot_here, w_key, w_value, ln_gain
        )
        return (carried + grads, embedded)

    scanned = (
        mem_rows.reshape(blocks, block_size, mem_width),
        query.reshape(blocks, block_size, mem_width),
        key_inputs.reshape(blocks, block_size, neighbors, key_inputs.shape[2]),
        cotangent.reshape(blocks, block_size, mem_width),
    )
    zero_grads = jnp.zeros((2, w_key.shape[0], mem_width), jnp.float32)
    grads, embedded = lax.scan(one_block, zero_grads, scanned)
    embedding = embedded.reshape(targets, mem_width).astype(jnp.bfloat16)[None]
    flat_grad = grads.reshape(-1)
    summed_grad = lax.psum(flat_grad, ("trainer", "store"))
    share_len = flat_grad.shape[0] // replicas
    my_index = lax.axis_index("trainer") * lax.axis_size("store") + lax.axis_index("store")
    grad_share = lax.dynamic_slice_in_dim(summed_grad, my_index * share_len, share_len)
    return (embedding, memory_next[None], grad_share)


def solution(mesh):
    placed = (
        P("store", None),
        P("store", None),
        P("trainer", "store"),
        P("trainer", "store"),
        P("trainer", "store", None, None),
        P("trainer", "store", None),
        P("trainer", "store", None),
        P(),
        P(),
        P(),
        P(),
        P(),
        P(),
        P(),
        P(),
        P("trainer", "store", None),
    )
    return jax.shard_map(
        on_device,
        mesh=mesh,
        in_specs=placed,
        out_specs=(
            P("trainer", "store", None),
            P("trainer", "store", None),
            P(("trainer", "store")),
        ),
        check_vma=False,
    )
```

profile of v0, /device:TPU:0, one launch (start us, length us, event | category | flops | bytes accessed | tf_op | source)
XLA Modules:
  0.0 341.5 jit_solution(2309487747094358767)
XLA Ops:
  14.2 6.5 %cosine_convert_fusion.1 = bf16[4,8,100,128]{3,2,1,0:T(8,128)(2,1)} fusion(f32[128]{0:T(128)S(1)} %copy-done.24, f32[128]{0:T(128)S(1)} %copy-done.25, f32[4,8,100]{2,1,0:T(8,128)S(1)} %fusion.49), kind=kLoop, calls=%fused_computation.52 | loop fusion | flops 1228800 | bytes 833024 | tf_op jit(solution)/shard_map/convert_element_type | solution.py:20
  20.7 6.5 %cosine_convert_fusion = bf16[32,100,128]{2,1,0:T(8,128)(2,1)} fusion(f32[128]{0:T(128)S(1)} %copy-done.24, f32[128]{0:T(128)S(1)} %copy-done.25, f32[32,100]{1,0:T(8,128)S(1)} %fusion.48), kind=kLoop, calls=%fused_computation.51 | loop fusion | flops 1228800 | bytes 833024 | tf_op jit(solution)/shard_map/convert_element_type | solution.py:20
  28.3 67.3 %all-gather.2.cloned.1.call-done = bf16[25600,128]{1,0:T(8,128)(2,1)} async-done(((bf16[12800,128]{1,0:T(8,128)(2,1)}), bf16[25600,128]{1,0:T(8,128)(2,1)}) %all-gather.2.cloned.1.call-update) | async-done | bytes 6553616 | tf_op jit(solution)/shard_map/all_gather | solution.py:121
  95.6 9.5 %gather_fusion = bf16[3200,128]{1,0:T(8,128)(2,1)S(1)} fusion(bf16[25600,128]{1,0:T(8,128)(2,1)} %all-gather.2.cloned.1.call-done, s32[4096]{0:T(1024)S(1)} %pad_clamp_fusion), kind=kCustom, calls=%fused_computation | custom fusion | bytes 1651200 | tf_op jit(solution)/shard_map/jit(_take)/gather | solution.py:126
  108.9 89.1 %while.14 = (s32[]{:T(128)}, f32[2,256,512]{2,1,0:T(8,128)}, bf16[4,8,512]{2,1,0:T(8,128)(2,1)S(1)}, bf16[4,8,100,256]{3,2,1,0:T(8,128)(2,1)}, f32[4,8,512]{2,1,...) while((s32[]{:T(128)}, f32[2,256,512]{2,1,0:T(8,128)}, ...), condition=%wide.wide.region_8.9_spmd.clone, body=%wide.wide.region_0.8_spmd.clone.sunk | while | flops 856556288 | bytes 24278400 | solution.py:159
  111.0 1.6 fusion.134
  113.3 2.9 fusion.135
  125.7 1.6 convolution_bitcast_fusion.8
  132.3 1.6 fusion.134
  134.7 2.9 fusion.135
  141.4 1.5 fusion.142
  147.1 1.6 convolution_bitcast_fusion.8
  150.4 2.4 maximum_add_fusion.3
  154.9 1.6 fusion.134
  157.3 2.9 fusion.135
  169.7 1.6 convolution_bitcast_fusion.8
  173.0 2.4 maximum_add_fusion.3
  177.5 1.6 fusion.134
  179.8 2.9 fusion.135
  192.3 1.6 convolution_bitcast_fusion.8
  195.6 2.4 maximum_add_fusion.3
  198.7 2.5 copy.39
  204.6 9.2 %collective-permute-done = f32[128,512]{1,0:T(8,128)S(1)} collective-permute-done((f32[128,512]{1,0:T(8,128)S(1)}, f32[128,512]{1,0:T(8,128)S(1)}, u32[]{:S(2)}, u32[]{:S(2)}) %collective-permute-start) | collective-permute-done | bytes 262176 | tf_op jit(solution)/shard_map/ppermute | solution.py:14
  213.7 118.9 %all-reduce.2.cloned.1.call-done = f32[262144]{0:T(1024)} async-done(((f32[262144]{0:T(1024)}), f32[262144]{0:T(1024)}) %all-reduce.2.cloned.1.call-update) | async-done | bytes 1048592 | tf_op jit(solution)/shard_map/psum | solution.py:162
  (274 shorter events, 72.9 us)
Async XLA Ops:
  7.2 20.1 %copy-start = (bf16[512,1536]{1,0:T(8,128)(2,1)S(1)}, bf16[512,1536]{1,0:T(8,128)(2,1)}, u32[]{:S(2)}) copy-start(bf16[512,1536]{1,0:T(8,128)(2,1)} %param.32) | copy-start | bytes 4718596
  7.2 88.4 %all-gather.2.cloned.1.call-start = ((), (), s32[]{:S(2)}) async-start(), calls=%async_computation | async-start | bytes 9830400 | tf_op jit(solution)/shard_map/all_gather | solution.py:121
  8.3 2.9 copy-start.5
  8.3 3.6 %copy-start.12 = (bf16[512,512]{1,0:T(8,128)(2,1)S(1)}, bf16[512,512]{1,0:T(8,128)(2,1)}, u32[]{:S(2)}) copy-start(bf16[512,512]{1,0:T(8,128)(2,1)} %param.27) | copy-start | bytes 1572868
  8.4 4.4 %copy-start.20 = (s32[1,32,100]{2,1,0:T(8,128)S(1)}, s32[1,32,100]{2,1,0:T(8,128)}, u32[]{:S(2)}) copy-start(s32[1,32,100]{2,1,0:T(8,128)} %param.24) | copy-start | bytes 38404
  8.4 5.2 %copy-start.21 = (bf16[1,32,512]{2,1,0:T(8,128)(2,1)S(1)}, bf16[1,32,512]{2,1,0:T(8,128)(2,1)}, u32[]{:S(2)}) copy-start(bf16[1,32,512]{2,1,0:T(8,128)(2,1)} %param.33) | copy-start | bytes 98308
  8.4 5.8 %copy-start.24 = (f32[128]{0:T(128)S(1)}, f32[128]{0:T(128)}, u32[]{:S(2)}) copy-start(f32[128]{0:T(128)} %param.26) | copy-start | bytes 1540
  8.4 5.8 %copy-start.25 = (f32[128]{0:T(128)S(1)}, f32[128]{0:T(128)}, u32[]{:S(2)}) copy-start(f32[128]{0:T(128)} %param.25) | copy-start | bytes 1540
  8.4 324.2 %all-reduce.2.cloned.1.call-start = ((), (), s32[]{:S(2)}) async-start(), calls=%async_computation.1 | async-start | bytes 2097152 | tf_op jit(solution)/shard_map/psum | solution.py:162
  11.8 16.5 %copy-start.7 = (f32[32,512]{1,0:T(8,128)}, f32[32,512]{1,0:T(8,128)S(1)}, u32[]{:S(2)}) copy-start(f32[32,512]{1,0:T(8,128)S(1)} %gather_fusion.1) | copy-start | bytes 196612
  108.9 11.0 %copy-start.18 = (f32[2,256]{1,0:T(2,128)}, f32[2,256]{1,0:T(2,128)S(1)}, u32[]{:S(2)}) copy-start(f32[2,256]{1,0:T(2,128)S(1)} %get-tuple-element.306) | copy-start | bytes 6148 | tf_op jit(solution)/shard_map/while
  113.3 3.7 %copy-start.1 = (f32[1,8,512]{2,1,0:T(8,128)}, f32[1,8,512]{2,1,0:T(8,128)S(1)}, u32[]{:S(2)}) copy-start(f32[1,8,512]{2,1,0:T(8,128)S(1)} %get-tuple-element.263) | copy-start | bytes 49156 | tf_op jit(solution)/shard_map/while
  130.3 11.0 %copy-start.18 = (f32[2,256]{1,0:T(2,128)}, f32[2,256]{1,0:T(2,128)S(1)}, u32[]{:S(2)}) copy-start(f32[2,256]{1,0:T(2,128)S(1)} %get-tuple-element.306) | copy-start | bytes 6148 | tf_op jit(solution)/shard_map/while
  134.6 3.7 %copy-start.1 = (f32[1,8,512]{2,1,0:T(8,128)}, f32[1,8,512]{2,1,0:T(8,128)S(1)}, u32[]{:S(2)}) copy-start(f32[1,8,512]{2,1,0:T(8,128)S(1)} %get-tuple-element.263) | copy-start | bytes 49156 | tf_op jit(solution)/shard_map/while
  150.4 2.5 copy-start.15
  152.9 11.0 %copy-start.18 = (f32[2,256]{1,0:T(2,128)}, f32[2,256]{1,0:T(2,128)S(1)}, u32[]{:S(2)}) copy-start(f32[2,256]{1,0:T(2,128)S(1)} %get-tuple-element.306) | copy-start | bytes 6148 | tf_op jit(solution)/shard_map/while
  157.2 3.7 %copy-start.1 = (f32[1,8,512]{2,1,0:T(8,128)}, f32[1,8,512]{2,1,0:T(8,128)S(1)}, u32[]{:S(2)}) copy-start(f32[1,8,512]{2,1,0:T(8,128)S(1)} %get-tuple-element.263) | copy-start | bytes 49156 | tf_op jit(solution)/shard_map/while
  173.0 2.5 copy-start.15
  175.4 11.0 %copy-start.18 = (f32[2,256]{1,0:T(2,128)}, f32[2,256]{1,0:T(2,128)S(1)}, u32[]{:S(2)}) copy-start(f32[2,256]{1,0:T(2,128)S(1)} %get-tuple-element.306) | copy-start | bytes 6148 | tf_op jit(solution)/shard_map/while
  179.8 3.7 %copy-start.1 = (f32[1,8,512]{2,1,0:T(8,128)}, f32[1,8,512]{2,1,0:T(8,128)S(1)}, u32[]{:S(2)}) copy-start(f32[1,8,512]{2,1,0:T(8,128)S(1)} %get-tuple-element.263) | copy-start | bytes 49156 | tf_op jit(solution)/shard_map/while
  198.0 3.1 copy-start.2
  198.1 3.1 copy-start.22
  198.1 3.1 copy-start.23
  204.5 9.3 %collective-permute-start = (f32[128,512]{1,0:T(8,128)S(1)}, f32[128,512]{1,0:T(8,128)S(1)}, u32[]{:S(2)}, u32[]{:S(2)}) collective-permute-start(f32[128,512]{1,0:T(8,128)S(1)} %scatter_custom_fusion), channel_id=1, source_target_pairs={{0,2},{2,4},{4,6},{6,8},{8,10},{10,12},{12,14},{14,16},{16,18},{18... | collective-permute-start | bytes 786440 | tf_op jit(solution)/shard_map/ppermute | solution.py:14
  (33 other events, 47.0 us)
Sparse Core Ops, SparseCore 0:
  9.5 86.0 all-gather.1
  201.3 131.2 all-reduce.1
where the time goes:
time: 343 us; the launch traced here: 342 us
  waiting for transfers between devices  195 us (57%)
  other arithmetic  48.4 us (14%)
  local copies, waits for them, and re-layouts  42.7 us (12%)
  matrix products  39.7 us (12%)
  between operations  14.4 us (4%)
    psum x1, waiting for transfers between devices, on_device(): summed_grad = lax.psum(flat_grad, ('trainer', 'store'))  119 us
    all_gather x1, waiting for transfers between devices, on_device(): shard_rows = lax.all_gather(event_feats, 'store', axis=0, tiled=True)  67.3 us
    convert_element_type x2, other arithmetic, key_inputs_of(): encoded.astype(jnp.bfloat16)  13.1 us
    dot_general x4, matrix products, attend_block(): jnp.einsum('bhd,bkhd->bhk', query_heads, key_rows, precision=highest)  11.7 us
    gather x3, local copies, waits for them, and re-layouts, on_device(): jnp.take(shard_rows, position, axis=0)  10.7 us
    ppermute x1, waiting for transfers between devices, passed_along(): return lax.ppermute(value, axis, pairs)  9.18 us
    add x4, other arithmetic, one_block(): return (carried + grads, embedded)  8.43 us
    unnamed x57, local copies, waits for them, and re-layouts  7.36 us
  transfers between devices with their start and end apart: 3, of which 3 were waited for; matrix products, arithmetic and copies ran while one was open for 6% of the time, Pallas kernels for 0%

commit v1 on v0

--- a/solution.py
+++ b/solution.py
@@ -118,7 +118,13 @@
     local_ids = neighbor_event.reshape(total_rows)
     wanted = owners * held_rows + local_ids
     blank_rows = jnp.zeros((total_rows, feat_width), jnp.bfloat16)
-    shard_rows = lax.all_gather(event_feats, "store", axis=0, tiled=True)
+    shard_rows = jnp.roll(
+        jnp.concatenate(
+            [event_feats, lax.ppermute(event_feats, "store", [(0, 1), (1, 0)])], axis=0
+        ),
+        lax.axis_index("store") * event_feats.shape[0],
+        axis=0,
+    )
     offset = jnp.int32(0)
     shard_len = shard_rows.shape[0]
     inside = (wanted >= offset) & (wanted < offset + shard_len)

time: 343 us -> 365 us (1.064)
  other arithmetic: 48.4 us -> 81.4 us
  waiting for transfers between devices: 195 us -> 179 us
    all_gather x1 -> x0, waiting for transfers between devices: 67.3 us -> none  [on_device(): shard_rows = lax.all_gather(event_feats, 'store', axis=0, tiled=True)]
    ppermute x0 -> x1, waiting for transfers between devices: none -> 47.5 us  [on_device(): lax.ppermute(event_feats, 'store', [(0, 1), (1, 0)])]
    concatenate x0 -> x1, other arithmetic: none -> 30.9 us  [on_device(): jnp.roll(jnp.concatenate([event_feats, lax.ppermute(event_feats, 'store',...]
    unnamed x57 -> x55, local copies, waits for them, and re-layouts: 7.36 us -> 7.84 us
  transfers between devices with their start and end apart: 3 -> 3, of which waited for: 3 -> 3; matrix products, arithmetic and copies ran while one was open for 6% -> 7% of each run, Pallas kernels for 0% -> 0%
where the time goes in v1:
time: 365 us; the launch traced here: 363 us
  waiting for transfers between devices  179 us (49%)
  other arithmetic  81.4 us (22%)
  local copies, waits for them, and re-layouts  44.7 us (12%)
  matrix products  39.7 us (11%)
  between operations  14.4 us (4%)
    psum x1, waiting for transfers between devices, on_device(): summed_grad = lax.psum(flat_grad, ('trainer', 'store'))  122 us
    ppermute x1, waiting for transfers between devices, on_device(): lax.ppermute(event_feats, 'store', [(0, 1), (1, 0)])  47.5 us
    concatenate x1, other arithmetic, on_device(): jnp.roll(jnp.concatenate([event_feats, lax.ppermute(event_feats, 'store',...  30.9 us
    convert_element_type x2, other arithmetic, key_inputs_of(): encoded.astype(jnp.bfloat16)  13.1 us
    dot_general x4, matrix products, attend_block(): jnp.einsum('bhd,bkhd->bhk', query_heads, key_rows, precision=highest)  11.7 us
    gather x3, local copies, waits for them, and re-layouts, on_device(): jnp.take(shard_rows, position, axis=0)  10.8 us
    add x4, other arithmetic, one_block(): return (carried + grads, embedded)  8.6 us
    ppermute x1, waiting for transfers between devices, passed_along(): return lax.ppermute(value, axis, pairs)  8.57 us
  transfers between devices with their start and end apart: 3, of which 3 were waited for; matrix products, arithmetic and copies ran while one was open for 7% of the time, Pallas kernels for 0%

profile of v1, /device:TPU:0, one launch (start us, length us, event | category | flops | bytes accessed | tf_op | source)
XLA Modules:
  0.0 362.7 jit_solution(7352561628250748361)
XLA Ops:
  8.4 3.0 collective-permute-start
  21.0 6.6 %cosine_convert_fusion.1 = bf16[4,8,100,128]{3,2,1,0:T(8,128)(2,1)} fusion(f32[128]{0:T(128)S(1)} %copy-done.24, f32[128]{0:T(128)S(1)} %copy-done.25, f32[4,8,100]{2,1,0:T(8,128)S(1)} %fusion.52), kind=kLoop, calls=%fused_computation.59 | loop fusion | flops 1228800 | bytes 833024 | tf_op jit(solution)/shard_map/convert_element_type | solution.py:20
  27.5 6.5 %cosine_convert_fusion = bf16[32,100,128]{2,1,0:T(8,128)(2,1)} fusion(f32[128]{0:T(128)S(1)} %copy-done.24, f32[128]{0:T(128)S(1)} %copy-done.25, f32[32,100]{1,0:T(8,128)S(1)} %fusion.51), kind=kLoop, calls=%fused_computation.58 | loop fusion | flops 1228800 | bytes 833024 | tf_op jit(solution)/shard_map/convert_element_type | solution.py:20
  35.1 47.5 %collective-permute-done = bf16[12800,128]{1,0:T(8,128)(2,1)} collective-permute-done((bf16[12800,128]{1,0:T(8,128)(2,1)}, bf16[12800,128]{1,0:T(8,128)(2,1)}, u32[]{:S(2)}, u32[]{:S(2)}) %collective-permute-start) | collective-permute-done | bytes 3276832 | tf_op jit(solution)/shard_map/ppermute | solution.py:123
  82.6 30.9 %fusion.26 = bf16[25600,128]{1,0:T(8,128)(2,1)} fusion(s32[]{:T(128)S(6)} %select_n.65, bf16[12800,128]{1,0:T(8,128)(2,1)S(1)} %copy-done.5, bf16[12800,128]{1,0:T(8,128)(2,1)} %collective-permute-done), kind=kLoop, calls=%fused_computation.56 | loop fusion | flops 26214400 | bytes 13107204 | tf_op jit(solution)/shard_map/jit(_roll_dynamic)/concatenate | solution.py:121
  113.5 9.6 %gather_fusion = bf16[3200,128]{1,0:T(8,128)(2,1)S(1)} fusion(bf16[25600,128]{1,0:T(8,128)(2,1)} %fusion.26, s32[4096]{0:T(1024)S(1)} %pad_clamp_fusion), kind=kCustom, calls=%fused_computation | custom fusion | bytes 1651200 | tf_op jit(solution)/shard_map/jit(_take)/gather | solution.py:132
  127.0 89.3 %while.14 = (s32[]{:T(128)}, f32[2,256,512]{2,1,0:T(8,128)}, bf16[4,8,512]{2,1,0:T(8,128)(2,1)S(1)}, bf16[4,8,100,256]{3,2,1,0:T(8,128)(2,1)}, f32[4,8,512]{2,1,...) while((s32[]{:T(128)}, f32[2,256,512]{2,1,0:T(8,128)}, ...), condition=%wide.wide.region_8.9_spmd.clone, body=%wide.wide.region_0.8_spmd.clone.sunk | while | flops 856556288 | bytes 24278400 | solution.py:165
  129.1 1.6 fusion.137
  131.4 2.9 fusion.138
  143.8 1.6 convolution_bitcast_fusion.8
  150.5 1.6 fusion.137
  152.8 2.9 fusion.138
  165.2 1.6 convolution_bitcast_fusion.8
  168.6 2.5 maximum_add_fusion.3
  173.1 1.6 fusion.137
  175.5 2.9 fusion.138
  187.9 1.6 convolution_bitcast_fusion.8
  191.2 2.5 maximum_add_fusion.3
  198.1 2.9 fusion.138
  210.5 1.6 convolution_bitcast_fusion.8
  213.8 2.5 maximum_add_fusion.3
  216.9 2.5 copy.39
  222.8 8.6 %collective-permute-done.1 = f32[128,512]{1,0:T(8,128)S(1)} collective-permute-done((f32[128,512]{1,0:T(8,128)S(1)}, f32[128,512]{1,0:T(8,128)S(1)}, u32[]{:S(2)}, u32[]{:S(2)}) %collective-permute-start.1) | collective-permute-done | bytes 262176 | tf_op jit(solution)/shard_map/ppermute | solution.py:14
  231.4 122.4 %all-reduce.2.cloned.1.call-done = f32[262144]{0:T(1024)} async-done(((f32[262144]{0:T(1024)}), f32[262144]{0:T(1024)}) %all-reduce.2.cloned.1.call-update) | async-done | bytes 1048592 | tf_op jit(solution)/shard_map/psum | solution.py:168
  (272 shorter events, 79.8 us)
Async XLA Ops:
  7.2 26.9 %copy-start = (bf16[512,1536]{1,0:T(8,128)(2,1)S(1)}, bf16[512,1536]{1,0:T(8,128)(2,1)}, u32[]{:S(2)}) copy-start(bf16[512,1536]{1,0:T(8,128)(2,1)} %param.32) | copy-start | bytes 4718596
  7.2 12.3 %copy-start.26 = (s32[1,32]{1,0:T(1,128)S(1)}, s32[1,32]{1,0:T(1,128)}, u32[]{:S(2)}) copy-start(s32[1,32]{1,0:T(1,128)} %param.21) | copy-start | bytes 388
  7.2 12.5 %copy-start.17 = (s32[1,32,100,1]{2,3,1,0:T(1,128)S(1)}, s32[1,32,100,1]{2,3,1,0:T(1,128)}, u32[]{:S(2)}) copy-start(s32[1,32,100,1]{2,3,1,0:T(1,128)} %param.22) | copy-start | bytes 38404
  7.2 12.5 %copy-start.16 = (s32[1,32,100]{2,1,0:T(8,128)S(1)}, s32[1,32,100]{2,1,0:T(8,128)}, u32[]{:S(2)}) copy-start(s32[1,32,100]{2,1,0:T(8,128)} %param.23) | copy-start | bytes 38404
  7.2 12.3 %copy-start.20 = (s32[1,32,100]{2,1,0:T(8,128)S(1)}, s32[1,32,100]{2,1,0:T(8,128)}, u32[]{:S(2)}) copy-start(s32[1,32,100]{2,1,0:T(8,128)} %param.24) | copy-start | bytes 38404
  7.2 13.7 %copy-start.25 = (f32[128]{0:T(128)S(1)}, f32[128]{0:T(128)}, u32[]{:S(2)}) copy-start(f32[128]{0:T(128)} %param.25) | copy-start | bytes 1540
  7.2 13.7 %copy-start.24 = (f32[128]{0:T(128)S(1)}, f32[128]{0:T(128)}, u32[]{:S(2)}) copy-start(f32[128]{0:T(128)} %param.26) | copy-start | bytes 1540
  7.2 11.4 %copy-start.13 = (bf16[512,512]{1,0:T(8,128)(2,1)S(1)}, bf16[512,512]{1,0:T(8,128)(2,1)}, u32[]{:S(2)}) copy-start(bf16[512,512]{1,0:T(8,128)(2,1)} %param.27) | copy-start | bytes 1572868
  7.3 13.1 %copy-start.21 = (bf16[1,32,512]{2,1,0:T(8,128)(2,1)S(1)}, bf16[1,32,512]{2,1,0:T(8,128)(2,1)}, u32[]{:S(2)}) copy-start(bf16[1,32,512]{2,1,0:T(8,128)(2,1)} %param.33) | copy-start | bytes 98308
  7.3 346.5 %all-reduce.2.cloned.1.call-start = ((), (), s32[]{:S(2)}) async-start(), calls=%async_computation | async-start | bytes 2097152 | tf_op jit(solution)/shard_map/psum | solution.py:168
  8.4 25.6 %copy-start.6 = (f32[128,512]{1,0:T(8,128)}, f32[128,512]{1,0:T(8,128)S(1)}, u32[]{:S(2)}) copy-start(f32[128,512]{1,0:T(8,128)S(1)} %copy.105) | copy-start | bytes 786436
  8.4 74.2 %collective-permute-start = (bf16[12800,128]{1,0:T(8,128)(2,1)}, bf16[12800,128]{1,0:T(8,128)(2,1)}, u32[]{:S(2)}, u32[]{:S(2)}) collective-permute-start(bf16[12800,128]{1,0:T(8,128)(2,1)} %param.19), channel_id=1, source_target_pairs={{0,1},{1,0},{2,3},{3,2},{4,5},{5,4},{6,7},{7,6},{8,9},{9,8},{10,11... | collective-permute-start | bytes 9830408 | tf_op jit(solution)/shard_map/ppermute | solution.py:123
  18.6 16.5 %copy-start.8 = (f32[32,512]{1,0:T(8,128)}, f32[32,512]{1,0:T(8,128)S(1)}, u32[]{:S(2)}) copy-start(f32[32,512]{1,0:T(8,128)S(1)} %gather_fusion.1) | copy-start | bytes 196612
  20.9 61.7 %copy-start.5 = (bf16[12800,128]{1,0:T(8,128)(2,1)S(1)}, bf16[12800,128]{1,0:T(8,128)(2,1)}, u32[]{:S(2)}) copy-start(bf16[12800,128]{1,0:T(8,128)(2,1)} %param.19) | copy-start | bytes 9830404
  127.0 11.0 %copy-start.18 = (f32[2,256]{1,0:T(2,128)}, f32[2,256]{1,0:T(2,128)S(1)}, u32[]{:S(2)}) copy-start(f32[2,256]{1,0:T(2,128)S(1)} %get-tuple-element.306) | copy-start | bytes 6148 | tf_op jit(solution)/shard_map/while
  131.4 3.7 %copy-start.1 = (f32[1,8,512]{2,1,0:T(8,128)}, f32[1,8,512]{2,1,0:T(8,128)S(1)}, u32[]{:S(2)}) copy-start(f32[1,8,512]{2,1,0:T(8,128)S(1)} %get-tuple-element.263) | copy-start | bytes 49156 | tf_op jit(solution)/shard_map/while
  148.4 11.1 %copy-start.18 = (f32[2,256]{1,0:T(2,128)}, f32[2,256]{1,0:T(2,128)S(1)}, u32[]{:S(2)}) copy-start(f32[2,256]{1,0:T(2,128)S(1)} %get-tuple-element.306) | copy-start | bytes 6148 | tf_op jit(solution)/shard_map/while
  152.8 3.7 %copy-start.1 = (f32[1,8,512]{2,1,0:T(8,128)}, f32[1,8,512]{2,1,0:T(8,128)S(1)}, u32[]{:S(2)}) copy-start(f32[1,8,512]{2,1,0:T(8,128)S(1)} %get-tuple-element.263) | copy-start | bytes 49156 | tf_op jit(solution)/shard_map/while
  171.0 11.1 %copy-start.18 = (f32[2,256]{1,0:T(2,128)}, f32[2,256]{1,0:T(2,128)S(1)}, u32[]{:S(2)}) copy-start(f32[2,256]{1,0:T(2,128)S(1)} %get-tuple-element.306) | copy-start | bytes 6148 | tf_op jit(solution)/shard_map/while
  175.4 3.7 %copy-start.1 = (f32[1,8,512]{2,1,0:T(8,128)}, f32[1,8,512]{2,1,0:T(8,128)S(1)}, u32[]{:S(2)}) copy-start(f32[1,8,512]{2,1,0:T(8,128)S(1)} %get-tuple-element.263) | copy-start | bytes 49156 | tf_op jit(solution)/shard_map/while
  193.7 11.1 %copy-start.18 = (f32[2,256]{1,0:T(2,128)}, f32[2,256]{1,0:T(2,128)S(1)}, u32[]{:S(2)}) copy-start(f32[2,256]{1,0:T(2,128)S(1)} %get-tuple-element.306) | copy-start | bytes 6148 | tf_op jit(solution)/shard_map/while
  198.1 3.7 %copy-start.1 = (f32[1,8,512]{2,1,0:T(8,128)}, f32[1,8,512]{2,1,0:T(8,128)S(1)}, u32[]{:S(2)}) copy-start(f32[1,8,512]{2,1,0:T(8,128)S(1)} %get-tuple-element.263) | copy-start | bytes 49156 | tf_op jit(solution)/shard_map/while
  216.3 3.1 copy-start.2
  222.7 8.6 %collective-permute-start.1 = (f32[128,512]{1,0:T(8,128)S(1)}, f32[128,512]{1,0:T(8,128)S(1)}, u32[]{:S(2)}, u32[]{:S(2)}) collective-permute-start(f32[128,512]{1,0:T(8,128)S(1)} %scatter_custom_fusion), channel_id=1, source_target_pairs={{0,2},{2,4},{4,6},{6,8},{8,10},{10,12},{12,14},{14,16},{16,18},{18... | collective-permute-start | bytes 786440 | tf_op jit(solution)/shard_map/ppermute | solution.py:14
  (32 other events, 50.2 us)
Sparse Core Ops, SparseCore 0:
  219.5 134.2 all-reduce.1
